TPU v7x, 128 devices: a whole 4x4x4 slice. The times are simulated.
128 devices in a mesh: row: 8 (over z, x_lo), col: 16 (over x_hi, y, core).
Axes of the slice: x: 4 (x_hi: 2, x_lo: 2; x = x_hi * 2 + x_lo), y: 4, z: 4, core: 2. Of those that a mesh axis runs over, the one named last changes fastest.
Arguments:
- tile_values: bfloat16 [8, 16, 256, 128, 128], P('row', 'col'), may hold values from -0.09375 to 0.09375
- tile_rows: int32 [8, 16, 256], P('row', 'col'), may hold values from 0 to 127
- tile_cols: int32 [8, 16, 256], P('row', 'col'), may hold values from 0 to 255
- increments: float32 [16, 128, 4096], P('row', None, 'col'), may hold values from 0 to 0.1
- dual_vars: float32 [16, 131072], P(None, 'row'), may hold values from 0 to 1
- flight_cost: float32 [128, 4096], P(None, 'col'), may hold values from -0.5 to 0.5
- win_start: int32 [4096], P('col'), may hold values from 0 to 63
- win_len: int32 [4096], P('col'), may hold values from 32 to 64
- capacity: int32 [16, 131072], P(None, 'row'), may hold values from 0 to 3
Outputs:
- primal: float32 [16, 128, 4096], P('row', None, 'col')
- duals_out: float32 [16, 131072], P(None, 'row')
Inputs may be any that keep to these rules, and one draw needn't show every extreme that they name: `tile_rows`: a block position may occur more than once in a device's list; such blocks add.
All inputs are finite; a program needn't handle non-finite values.
Results may differ from a plain program's by a relative error of at most 0.0056.
Values may be sent and summed in bfloat16 or wider, within the bound.
A program may use at most 64 MiB of HBM per device.

v0:
```python
import math

import jax
import jax.numpy as jnp
from jax import lax
from jax.sharding import PartitionSpec as P

ITERS = 2


SIGMA_STEP = 0.2


def running_total(values):
    length = values.shape[1]
    row_iota = lax.broadcasted_iota(jnp.int32, (length, length), 0)
    col_iota = lax.broadcasted_iota(jnp.int32, (length, length), 1)
    triangle = (row_iota >= col_iota).astype(jnp.float32)
    return jnp.einsum("kj,sjf->skf", triangle, values, precision=lax.Precision.HIGHEST)


def trailing_total(values):
    length = values.shape[1]
    row_iota = lax.broadcasted_iota(jnp.int32, (length, length), 0)
    col_iota = lax.broadcasted_iota(jnp.int32, (length, length), 1)
    triangle = (row_iota >= col_iota).astype(jnp.float32)
    return jnp.einsum("jk,sjf->skf", triangle, values, precision=lax.Precision.HIGHEST)


def per_device(
    tile_values,
    tile_rows,
    tile_cols,
    increments,
    dual_vars,
    flight_cost,
    win_start,
    win_len,
    capacity,
):
    n_col = lax.axis_size("col")
    tile_count = tile_values.shape[2]
    tile_side = tile_values.shape[3]
    blocks = tile_values.reshape(tile_count, tile_side, tile_side)
    row_index = tile_rows.reshape(tile_count)
    col_index = tile_cols.reshape(tile_count)
    scen_local, window, flight_local = increments.shape
    tau_step = 0.6 / math.sqrt(window)
    scenarios, row_length = dual_vars.shape
    row_tiles = row_length // tile_side
    time_block = window // n_col
    flights = flight_local * n_col
    col_tiles = time_block * flights // tile_side
    hot_rows = (
        row_index[None, :] == lax.broadcasted_iota(jnp.int32, (row_tiles, tile_count), 0)
    ).astype(jnp.float32)
    hot_cols = (
        col_index[None, :] == lax.broadcasted_iota(jnp.int32, (col_tiles, tile_count), 0)
    ).astype(jnp.float32)
    minutes = lax.broadcasted_iota(jnp.int32, (window, flight_local), 0)
    upper_bound = (
        (minutes >= win_start[None, :]) & (minutes < (win_start + win_len)[None, :])
    ).astype(jnp.float32)
    capacity_f = capacity.astype(jnp.float32)
    current = dual_vars
    primal = increments
    cumulative = running_total(primal)
    for sweep_index in range(ITERS):
        dual_blocks = current.astype(jnp.bfloat16).reshape(scenarios, row_tiles, tile_side)
        picked = jnp.take(dual_blocks, row_index, axis=1)
        products = jnp.einsum("nij,sni->snj", blocks, picked, preferred_element_type=jnp.float32)
        summed = lax.psum_scatter(
            jnp.einsum("cn,snj->scj", hot_cols, products, precision=lax.Precision.HIGHEST),
            "row",
            scatter_dimension=0,
            tiled=True,
        )
        slope_tb = summed.reshape(scen_local, time_block, flights)
        flight_slope = lax.all_to_all(slope_tb, "col", split_axis=2, concat_axis=1, tiled=True)
        gradient = trailing_total(flight_slope + flight_cost[None])
        primal = jnp.clip(primal - tau_step * gradient, 0.0, upper_bound[None])
        fresh_sum = running_total(primal)
        probe_fc = (2.0 * fresh_sum - cumulative).astype(jnp.bfloat16)
        probe_vec = lax.all_to_all(probe_fc, "col", split_axis=1, concat_axis=2, tiled=True)
        gathered_part = lax.all_gather(probe_vec, "row", axis=0, tiled=True)
        probe_blocks = gathered_part.reshape(gathered_part.shape[0], col_tiles, tile_side)
        image_picked = jnp.take(probe_blocks, col_index, axis=1)
        image_products = jnp.einsum(
            "nij,snj->sni", blocks, image_picked, preferred_element_type=jnp.float32
        )
        partial_value = jnp.einsum(
            "rn,sni->sri", hot_rows, image_products, precision=lax.Precision.HIGHEST
        )
        flattened = partial_value.reshape(scenarios, row_length)
        col_total = lax.psum(flattened, "col")
        current = jnp.maximum(current + SIGMA_STEP * (col_total - capacity_f), 0.0)
        cumulative = fresh_sum
    return (primal, current)


def solution(mesh):
    placed = (
        P("row", "col", None, None, None),
        P("row", "col", None),
        P("row", "col", None),
        P("row", None, "col"),
        P(None, "row"),
        P(None, "col"),
        P("col"),
        P("col"),
        P(None, "row"),
    )
    return jax.shard_map(
        per_device,
        mesh=mesh,
        in_specs=placed,
        out_specs=(P("row", None, "col"), P(None, "row")),
        check_vma=False,
    )
```

profile of v0, /device:TPU:1, one launch (start us, length us, event | category | flops | bytes accessed | tf_op | source)
XLA Modules:
  0.0 658.8 jit_solution(13502847819924775198)
XLA Ops:
  10.7 4.7 fusion.22
  19.0 55.9 %reduce-scatter.3.cloned.1.call-done = f32[2,256,128]{1,2,0:T(8,128)} async-done(((f32[16,256,128]{1,2,0:T(8,128)}), f32[2,256,128]{1,2,0:T(8,128)}) %reduce-scatter.3.cloned.1.call-update) | async-done | bytes 262160 | tf_op jit(solution)/shard_map/reduce_scatter | solution.py:72
  76.0 4.3 copy.52
  80.3 9.0 %reshape.143 = f32[16,1,4096]{2,1,0:T(1,128)} reshape(f32[4096,2,8]{2,1,0:T(2,128)} %bitcast.137) | data formatting | bytes 524288
  89.3 7.2 %all-to-all-start = ((f32[16,1,4096]{2,1,0:T(1,128)}), f32[16,1,4096]{2,1,0:T(1,128)S(1)}, u32[]{:S(2)}, u32[]{:S(2)}) async-start(f32[16,1,4096]{2,1,0:T(1,128)} %reshape.143), calls=%async_computation.1 | async-start | bytes 524288 | tf_op jit(solution)/shard_map/all_to_all | solution.py:79
  96.9 8.3 %all-to-all-done = f32[16,1,4096]{2,1,0:T(1,128)S(1)} async-done(((f32[16,1,4096]{2,1,0:T(1,128)}), f32[16,1,4096]{2,1,0:T(1,128)S(1)}, u32[]{:S(2)}, u32[]{:S(2)}) %all-to-all-start) | async-done | bytes 262176 | tf_op jit(solution)/shard_map/all_to_all | solution.py:79
  107.1 7.7 %reshape.144 = f32[4096,2,8]{2,1,0:T(2,128)} reshape(f32[16,4096]{1,0:T(8,128)S(1)} %reduce) | data formatting | bytes 524288
  114.7 5.2 copy.80
  121.2 11.1 %all_to_all.72 = bf16[2,128,256]{2,0,1:T(2,128)(2,1)S(1)} all-to-all(bf16[2,128,256]{2,0,1:T(2,128)(2,1)S(1)} %copy.58), channel_id=1, replica_groups=mesh['row'=8,'col'=16] {'col'}, dimensions={1} | all-to-all | bytes 262144 | tf_op jit(solution)/shard_map/all_to_all | solution.py:84
  133.2 31.2 %all-gather.3.cloned.1.call-done = bf16[16,8,4096]{2,1,0:T(8,128)(2,1)} async-done(((bf16[2,8,4096]{2,1,0:T(8,128)(2,1)}), bf16[16,8,4096]{2,1,0:T(8,128)(2,1)}) %all-gather.3.cloned.1.call-update) | async-done | bytes 1048592 | tf_op jit(solution)/shard_map/all_gather | solution.py:85
  167.5 6.9 %fusion.25 = f32[16,256,128]{2,0,1:T(8,128)S(1)} fusion(bf16[1,1,256,128,128]{4,3,2,1,0:T(8,128)(2,1)} %param.13, bf16[256,16,128]{2,1,0:T(8,128)(2,1)S(1)} %gather_fusion.1, pred[256]{0:T(512)(128)(4,1)S(1)} %compare_and_fusion), kind=kOutput, calls=%fused_computation.23 | convolution fusion | flops 134742016 | bytes 11534592 | tf_op jit(solution)/shard_map/nij,snj->sni/dot_general | solution.py:88
  180.8 144.4 %all-reduce.3.cloned.1.call-done = f32[16,16384]{1,0:T(8,128)} async-done(((f32[16,16384]{1,0:T(8,128)}), f32[16,16384]{1,0:T(8,128)}) %all-reduce.3.cloned.1.call-update) | async-done | bytes 1048592 | tf_op jit(solution)/shard_map/psum | solution.py:95
  328.4 6.1 fusion.28
  334.4 3.5 fusion.19
  338.2 53.6 %reduce-scatter.5.cloned.1.call-done = f32[2,256,128]{1,2,0:T(8,128)} async-done(((f32[16,256,128]{1,2,0:T(8,128)}), f32[2,256,128]{1,2,0:T(8,128)}) %reduce-scatter.5.cloned.1.call-update) | async-done | bytes 262160 | tf_op jit(solution)/shard_map/reduce_scatter | solution.py:72
  392.9 4.3 copy.66
  397.2 8.3 %reshape.145 = f32[16,1,4096]{2,1,0:T(1,128)S(1)} reshape(f32[4096,2,8]{2,1,0:T(2,128)} %bitcast.139) | data formatting | bytes 524288
  405.5 15.7 %all_to_all.73 = f32[16,1,4096]{2,1,0:T(1,128)S(1)} all-to-all(f32[16,1,4096]{2,1,0:T(1,128)S(1)} %reshape.145), channel_id=1, replica_groups=mesh['row'=8,'col'=16] {'col'}, dimensions={0} | all-to-all | bytes 524288 | tf_op jit(solution)/shard_map/all_to_all | solution.py:79
  422.5 7.7 %reshape.146 = f32[4096,2,8]{2,1,0:T(2,128)} reshape(f32[16,4096]{1,0:T(8,128)S(1)} %reduce.1) | data formatting | bytes 524288
  430.2 5.1 copy.82
  436.2 11.1 %all_to_all.74 = bf16[2,128,256]{2,0,1:T(2,128)(2,1)S(1)} all-to-all(bf16[2,128,256]{2,0,1:T(2,128)(2,1)S(1)} %copy.70), channel_id=1, replica_groups=mesh['row'=8,'col'=16] {'col'}, dimensions={1} | all-to-all | bytes 262144 | tf_op jit(solution)/shard_map/all_to_all | solution.py:84
  448.3 31.1 %all-gather.5.cloned.1.call-done = bf16[16,8,4096]{2,1,0:T(8,128)(2,1)} async-done(((bf16[2,8,4096]{2,1,0:T(8,128)(2,1)}), bf16[16,8,4096]{2,1,0:T(8,128)(2,1)}) %all-gather.5.cloned.1.call-update) | async-done | bytes 1048592 | tf_op jit(solution)/shard_map/all_gather | solution.py:85
  487.6 8.2 %fusion.31 = f32[16,256,128]{2,0,1:T(8,128)S(1)} fusion(bf16[1,1,256,128,128]{4,3,2,1,0:T(8,128)(2,1)} %param.13, bf16[256,16,128]{2,1,0:T(8,128)(2,1)} %gather_fusion.3, pred[256]{0:T(512)(128)(4,1)S(1)} %compare_and_fusion), kind=kOutput, calls=%fused_computation.25 | convolution fusion | flops 134742016 | bytes 11534592 | tf_op jit(solution)/shard_map/nij,snj->sni/dot_general | solution.py:88
  505.1 143.6 %all-reduce.5.cloned.1.call-done = f32[16,16384]{1,0:T(8,128)} async-done(((f32[16,16384]{1,0:T(8,128)}), f32[16,16384]{1,0:T(8,128)}) %all-reduce.5.cloned.1.call-update) | async-done | bytes 1048592 | tf_op jit(solution)/shard_map/psum | solution.py:95
  (72 shorter events, 50.0 us)
Async XLA Ops:
  7.2 67.7 %reduce-scatter.3.cloned.1.call-start = ((), (), s32[]{:S(2)}) async-start(), calls=%async_computation.6 | async-start | bytes 2359296 | tf_op jit(solution)/shard_map/reduce_scatter | solution.py:72
  10.7 4.8 copy-start.4
  80.3 16.3 %copy-start.2 = (f32[2,128,256]{2,1,0:T(8,128)S(1)}, f32[2,128,256]{2,1,0:T(8,128)}, u32[]{:S(2)}) copy-start(f32[2,128,256]{2,1,0:T(8,128)} %param.16) | copy-start | bytes 786436
  80.3 16.4 %copy-start.6 = (s32[256]{0:T(256)S(1)}, s32[256]{0:T(256)}, u32[]{:S(2)}) copy-start(s32[256]{0:T(256)} %param.19) | copy-start | bytes 3076
  80.3 16.4 %copy-start.7 = (s32[256]{0:T(256)S(1)}, s32[256]{0:T(256)}, u32[]{:S(2)}) copy-start(s32[256]{0:T(256)} %param.20) | copy-start | bytes 3076
  89.3 15.9 %all-to-all-start = ((f32[16,1,4096]{2,1,0:T(1,128)}), f32[16,1,4096]{2,1,0:T(1,128)S(1)}, u32[]{:S(2)}, u32[]{:S(2)}) async-start(f32[16,1,4096]{2,1,0:T(1,128)} %reshape.143), calls=%async_computation.1 | async-start | bytes 524288 | tf_op jit(solution)/shard_map/all_to_all | solution.py:79
  96.5 67.9 %all-gather.3.cloned.1.call-start = ((), (), s32[]{:S(2)}) async-start(), calls=%async_computation.7 | async-start | bytes 1179648 | tf_op jit(solution)/shard_map/all_gather | solution.py:85
  114.7 5.2 copy-start.3
  133.0 192.2 %all-reduce.3.cloned.1.call-start = ((), (), s32[]{:S(2)}) async-start(), calls=%async_computation.8 | async-start | bytes 2097152 | tf_op jit(solution)/shard_map/psum | solution.py:95
  167.5 6.9 %copy-start.5 = (s32[1,1,256]{2,1,0:T(1,128)S(1)}, s32[1,1,256]{2,1,0:T(1,128)}, u32[]{:S(2)}) copy-start(s32[1,1,256]{2,1,0:T(1,128)} %param.14) | copy-start | bytes 3076
  177.8 147.4 %copy-start = (f32[16,16384]{1,0:T(8,128)S(1)}, f32[16,16384]{1,0:T(8,128)}, u32[]{:S(2)}) copy-start(f32[16,16384]{1,0:T(8,128)} %param.17) | copy-start | bytes 3145732
  177.8 147.4 %copy-start.1 = (s32[16,16384]{1,0:T(8,128)S(1)}, s32[16,16384]{1,0:T(8,128)}, u32[]{:S(2)}) copy-start(s32[16,16384]{1,0:T(8,128)} %param.21) | copy-start | bytes 3145732
  180.8 211.0 %reduce-scatter.5.cloned.1.call-start = ((), (), s32[]{:S(2)}) async-start(), calls=%async_computation.9 | async-start | bytes 2359296 | tf_op jit(solution)/shard_map/reduce_scatter | solution.py:72
  337.9 141.5 %all-gather.5.cloned.1.call-start = ((), (), s32[]{:S(2)}) async-start(), calls=%async_computation.10 | async-start | bytes 1179648 | tf_op jit(solution)/shard_map/all_gather | solution.py:85
  448.0 200.7 %all-reduce.5.cloned.1.call-start = ((), (), s32[]{:S(2)}) async-start(), calls=%async_computation.11 | async-start | bytes 2097152 | tf_op jit(solution)/shard_map/psum | solution.py:95
Sparse Core Ops, SparseCore 0:
  19.1 55.6 reduce-scatter.2
  133.1 31.2 all-gather.2
  180.9 144.2 all-reduce.2
  338.1 53.6 reduce-scatter.4
  448.1 31.2 all-gather.4
  504.4 144.2 all-reduce.4
where the time goes:
time: 668 us; the launch traced here: 659 us
  waiting for transfers between devices  468 us (70%)
  local copies, waits for them, and re-layouts  80.4 us (12%)
  matrix products  39.8 us (6%)
  blocking collectives  38 us (6%)
  between operations  14.8 us (2%)
  other arithmetic  9.65 us (1%)
  starting transfers between devices  8.12 us (1%)
    psum x2, waiting for transfers between devices, per_device(): col_total = lax.psum(flattened, 'col')  288 us
    reduce_scatter x2, waiting for transfers between devices, per_device(): lax.psum_scatter(jnp.einsum('cn,snj->scj', hot_cols, products, precision=...  109 us
    all_gather x2, waiting for transfers between devices, per_device(): gathered_part = lax.all_gather(probe_vec, 'row', axis=0, tiled=True)  62.3 us
    unnamed x24, local copies, waits for them, and re-layouts  39.3 us
    all_to_all x2, blocking collectives, per_device(): lax.all_to_all(probe_fc, 'col', split_axis=1, concat_axis=2, tiled=True)  22.2 us
    all_to_all x1, blocking collectives, per_device(): lax.all_to_all(slope_tb, 'col', split_axis=2, concat_axis=1, tiled=True)  15.7 us
    dot_general x2, matrix products, per_device(): jnp.einsum('nij,snj->sni', blocks, image_picked, preferred_element_type=j...  15.1 us
  transfers between devices with their start and end apart: 7, of which 7 were waited for; matrix products, arithmetic and copies ran while one was open for 0% of the time, Pallas kernels for 0%

commit v1 on v0

v1 whole, which is shorter than its diff:
```python
import functools
import math

import jax
import jax.numpy as jnp
from jax import lax
from jax.experimental import pallas as pl
from jax.experimental.pallas import tpu as pltpu
from jax.sharding import PartitionSpec as P

ITERS = 2
SIGMA_STEP = 0.2
MESH = pl.DeviceIdType.MESH
F32, BF16 = jnp.float32, jnp.bfloat16
LOAD_CHUNKS = 8


def kernel(
    dims,
    values_hbm,
    row_of,
    col_of,
    row_vec,
    col_vec,
    inc_ref,
    dual_ref,
    cost_ref,
    start_ref,
    len_ref,
    cap_ref,
    primal_ref,
    duals_ref,
    blocks,
    hot_cols,
    hot_rows,
    products,
    by_tile,
    slope_send,
    slope_recv,
    slope,
    cumulative,
    probe_send,
    probe_recv,
    image_send,
    image_recv,
    own_dual,
    own_cap,
    own_send,
    duals_recv,
    load_sem,
    local_sem,
    send_sem,
    slope_sem,
    probe_sem,
    row_send_sem,
    image_sem,
    dual_sem,
):
    n_row, n_col, scenarios, scen_local, window, tiles, row_tiles, col_tiles = dims
    devices = n_row * n_col
    block_rows = 16
    per_load = tiles // LOAD_CHUNKS
    picked = by_tile.reshape(by_tile.shape[0] * scenarios, by_tile.shape[2])
    tau_step = 0.6 / math.sqrt(window)
    me_r, me_c = lax.axis_index("row"), lax.axis_index("col")
    me = me_r * n_col + me_c

    def load(chunk):
        span = pl.ds(chunk * per_load, per_load)
        return pltpu.make_async_copy(
            values_hbm.at[span], blocks.at[span], load_sem.at[chunk]
        )

    for chunk in range(LOAD_CHUNKS):
        load(chunk).start()

    def peer_of(step):
        peer = lax.rem(me + step, devices)
        return peer, peer // n_col, lax.rem(peer, n_col)

    barrier = pltpu.get_barrier_semaphore()

    @pl.loop(1, devices)
    def _(step):
        _, peer_r, peer_c = peer_of(step)
        pl.semaphore_signal(barrier, inc=1, device_id=(peer_r, peer_c), device_id_type=MESH)

    def slope_copy(peer_r, peer_c):
        return pltpu.make_async_remote_copy(
            src_ref=slope_send.at[
                pl.ds(peer_r * scen_local, scen_local),
                pl.ds(pl.multiple_of(peer_c * block_rows, block_rows), block_rows),
            ],
            dst_ref=slope_recv.at[me],
            send_sem=send_sem.at[peer_r * n_col + peer_c],
            recv_sem=slope_sem.at[me],
            device_id=(peer_r, peer_c),
            device_id_type=MESH,
        )

    def slope_arrival(peer, peer_r, peer_c):
        return pltpu.make_async_remote_copy(
            src_ref=slope_recv.at[peer],
            dst_ref=slope_recv.at[peer],
            send_sem=send_sem.at[peer],
            recv_sem=slope_sem.at[peer],
            device_id=(peer_r, peer_c),
            device_id_type=MESH,
        )

    def probe_place(r, c):
        return probe_recv.at[
            pl.ds(r * scen_local, scen_local),
            pl.ds(pl.multiple_of(c * block_rows, block_rows), block_rows),
        ]

    def probe_copy(peer_r, peer_c):
        return pltpu.make_async_remote_copy(
            src_ref=probe_send.at[peer_c],
            dst_ref=probe_place(me_r, me_c),
            send_sem=send_sem.at[peer_r * n_col + peer_c],
            recv_sem=probe_sem.at[me],
            device_id=(peer_r, peer_c),
            device_id_type=MESH,
        )

    def probe_arrival(peer, peer_r, peer_c):
        return pltpu.make_async_remote_copy(
            src_ref=probe_place(peer_r, peer_c),
            dst_ref=probe_place(peer_r, peer_c),
            send_sem=send_sem.at[peer],
            recv_sem=probe_sem.at[peer],
            device_id=(peer_r, peer_c),
            device_id_type=MESH,
        )

    def image_copy(peer_c):
        return pltpu.make_async_remote_copy(
            src_ref=image_send.at[peer_c],
            dst_ref=image_recv.at[me_c],
            send_sem=row_send_sem.at[peer_c],
            recv_sem=image_sem.at[me_c],
            device_id=(me_r, peer_c),
            device_id_type=MESH,
        )

    def image_arrival(peer_c):
        return pltpu.make_async_remote_copy(
            src_ref=image_recv.at[peer_c],
            dst_ref=image_recv.at[peer_c],
            send_sem=row_send_sem.at[peer_c],
            recv_sem=image_sem.at[peer_c],
            device_id=(me_r, peer_c),
            device_id_type=MESH,
        )

    def dual_copy(peer_c):
        return pltpu.make_async_remote_copy(
            src_ref=own_send,
            dst_ref=duals_recv.at[me_c],
            send_sem=row_send_sem.at[peer_c],
            recv_sem=dual_sem.at[me_c],
            device_id=(me_r, peer_c),
            device_id_type=MESH,
        )

    def dual_arrival(peer_c):
        return pltpu.make_async_remote_copy(
            src_ref=duals_recv.at[peer_c],
            dst_ref=duals_recv.at[peer_c],
            send_sem=row_send_sem.at[peer_c],
            recv_sem=dual_sem.at[peer_c],
            device_id=(me_r, peer_c),
            device_id_type=MESH,
        )

    hot_cols[...] = (
        col_vec[...] == lax.broadcasted_iota(jnp.int32, (col_tiles, tiles), 0)
    ).astype(F32).astype(BF16)
    hot_rows[...] = (
        row_vec[...] == lax.broadcasted_iota(jnp.int32, (row_tiles, tiles), 0)
    ).astype(F32).astype(BF16)

    @pl.loop(0, row_tiles)
    def _(tile):
        lanes = pl.ds(pl.multiple_of(tile * 128, 128), 128)
        rows = pl.ds(pl.multiple_of(tile * scenarios, scenarios), scenarios)
        products[rows, :] = cap_ref[:, lanes].astype(F32)
        picked[rows, :] = dual_ref[:, lanes]

    own_cap[...] = products[pl.ds(me_c, row_tiles, stride=scenarios), :]
    own_dual[...] = picked[pl.ds(me_c, row_tiles, stride=scenarios), :]

    row_iota = lax.broadcasted_iota(jnp.int32, (window, window), 0)
    col_iota = lax.broadcasted_iota(jnp.int32, (window, window), 1)
    running = (row_iota >= col_iota).astype(F32)
    trailing = (row_iota <= col_iota).astype(F32)
    flights = inc_ref.shape[2]

    def total(triangle, values):
        return jnp.dot(
            triangle, values, precision=lax.Precision.HIGHEST, preferred_element_type=F32
        )

    for scen in range(scen_local):
        primal_ref[scen] = inc_ref[scen]
        cumulative[scen] = total(running, inc_ref[scen])
    minutes = lax.broadcasted_iota(jnp.int32, (window, flights), 0)
    upper = (
        (minutes >= start_ref[...]) & (minutes < start_ref[...] + len_ref[...])
    ).astype(F32)

    for sweep in range(ITERS):
        for chunk in range(LOAD_CHUNKS):
            if sweep == 0:
                load(chunk).wait()

            @pl.loop(0, per_load // 8)
            def _(group):
                for k in range(8):
                    n = chunk * per_load + group * 8 + k
                    products[pl.ds(pl.multiple_of(n * scenarios, scenarios), scenarios), :] = (
                        jnp.dot(
                            by_tile[row_of[n]].astype(BF16),
                            blocks[n],
                            preferred_element_type=F32,
                        )
                    )

        if sweep == 0:
            pl.semaphore_wait(barrier, devices - 1)

        for group in range(n_row):
            for scen in range(group * scen_local, (group + 1) * scen_local):
                taken = products[pl.ds(scen, tiles, stride=scenarios), :].astype(BF16)
                slope_send[scen] = jnp.dot(
                    hot_cols[...], taken, preferred_element_type=F32
                ).astype(BF16)

        own = pltpu.make_async_copy(
            slope_send.at[
                pl.ds(me_r * scen_local, scen_local),
                pl.ds(pl.multiple_of(me_c * block_rows, block_rows), block_rows),
            ],
            slope_recv.at[me],
            local_sem.at[0],
        )
        own.start()

        @pl.loop(1, devices)
        def _(step):
            _, peer_r, peer_c = peer_of(step)
            slope_copy(peer_r, peer_c).start()

        own.wait()

        @pl.loop(1, devices)
        def _(step):
            peer, peer_r, peer_c = peer_of(devices - step)
            slope_arrival(peer, peer_r, peer_c).wait_recv()

        @pl.loop(0, n_col)
        def _(part):
            summed = slope_recv[part].astype(F32)
            for group in range(1, n_row):
                summed = summed + slope_recv[group * n_col + part].astype(F32)
            rows = pl.ds(pl.multiple_of(part * 8, 8), 8)
            for scen in range(scen_local):
                for half in range(flights // 128):
                    lanes = slice(half * 128, (half + 1) * 128)
                    slope[scen, rows, lanes] = (
                        summed[scen, half * 8 : (half + 1) * 8] + cost_ref[rows, lanes]
                    )

        @pl.loop(1, devices)
        def _(step):
            _, peer_r, peer_c = peer_of(step)
            slope_copy(peer_r, peer_c).wait_send()

        for scen in range(scen_local):
            gradient = total(trailing, slope[scen])
            fresh = jnp.clip(primal_ref[scen] - tau_step * gradient, 0.0, upper)
            primal_ref[scen] = fresh
            fresh_sum = total(running, fresh)
            probe = 2.0 * fresh_sum - cumulative[scen]
            cumulative[scen] = fresh_sum
            for part in range(n_col):
                probe_send[part, scen] = jnp.concatenate(
                    [
                        probe[part * 8 : (part + 1) * 8, half * 128 : (half + 1) * 128]
                        for half in range(flights // 128)
                    ],
                    axis=0,
                ).astype(BF16)

        own = pltpu.make_async_copy(
            probe_send.at[me_c], probe_place(me_r, me_c), local_sem.at[0]
        )
        own.start()

        @pl.loop(1, devices)
        def _(step):
            _, peer_r, peer_c = peer_of(step)
            probe_copy(peer_r, peer_c).start()

        own.wait()

        @pl.loop(1, devices)
        def _(step):
            peer, peer_r, peer_c = peer_of(devices - step)
            probe_arrival(peer, peer_r, peer_c).wait_recv()

        for scen in range(scenarios):
            picked[pl.ds(scen, col_tiles, stride=scenarios), :] = probe_recv[scen].astype(F32)

        @pl.loop(1, devices)
        def _(step):
            _, peer_r, peer_c = peer_of(step)
            probe_copy(peer_r, peer_c).wait_send()

        @pl.loop(0, tiles // 8)
        def _(group):
            for k in range(8):
                n = group * 8 + k
                products[pl.ds(pl.multiple_of(n * scenarios, scenarios), scenarios), :] = (
                    lax.dot_general(
                        by_tile[col_of[n]].astype(BF16),
                        blocks[n],
                        (((1,), (1,)), ((), ())),
                        preferred_element_type=F32,
                    )
                )

        for scen in range(scenarios):
            taken = products[pl.ds(scen, tiles, stride=scenarios), :].astype(BF16)
            image_send[scen] = jnp.dot(
                hot_rows[...], taken, preferred_element_type=F32
            ).astype(BF16)

        own = pltpu.make_async_copy(
            image_send.at[me_c], image_recv.at[me_c], local_sem.at[0]
        )
        own.start()

        @pl.loop(1, n_col)
        def _(step):
            image_copy(lax.rem(me_c + step, n_col)).start()

        own.wait()

        @pl.loop(1, n_col)
        def _(step):
            image_arrival(lax.rem(me_c + n_col - step, n_col)).wait_recv()

        image = image_recv[0].astype(F32)
        for part in range(1, n_col):
            image = image + image_recv[part].astype(F32)
        updated = jnp.maximum(own_dual[...] + SIGMA_STEP * (image - own_cap[...]), 0.0)
        own_dual[...] = updated
        own_send[...] = updated.astype(BF16)

        @pl.loop(1, n_col)
        def _(step):
            image_copy(lax.rem(me_c + step, n_col)).wait_send()

        own = pltpu.make_async_copy(own_send, duals_recv.at[me_c], local_sem.at[0])
        own.start()

        @pl.loop(1, n_col)
        def _(step):
            dual_copy(lax.rem(me_c + step, n_col)).start()

        own.wait()

        @pl.loop(1, n_col)
        def _(step):
            dual_arrival(lax.rem(me_c + n_col - step, n_col)).wait_recv()

        for scen in range(scenarios):
            picked[pl.ds(scen, row_tiles, stride=scenarios), :] = duals_recv[scen].astype(F32)

        @pl.loop(1, n_col)
        def _(step):
            dual_copy(lax.rem(me_c + step, n_col)).wait_send()

    @pl.loop(0, row_tiles)
    def _(tile):
        duals_ref[:, pl.ds(pl.multiple_of(tile * 128, 128), 128)] = picked[
            pl.ds(pl.multiple_of(tile * scenarios, scenarios), scenarios), :
        ]


def per_device(
    tile_values,
    tile_rows,
    tile_cols,
    increments,
    dual_vars,
    flight_cost,
    win_start,
    win_len,
    capacity,
):
    n_row, n_col = lax.axis_size("row"), lax.axis_size("col")
    tiles, side = tile_values.shape[2], tile_values.shape[3]
    scen_local, window, flight_local = increments.shape
    scenarios, row_length = dual_vars.shape
    row_tiles = row_length // side
    time_block = window // n_col
    flight_tiles = flight_local * n_col // side
    col_tiles = time_block * flight_tiles
    assert scenarios == n_col and time_block == 8 and flight_local == 256
    devices = n_row * n_col
    row_index = tile_rows.reshape(tiles)
    col_index = tile_cols.reshape(tiles)
    col_place = lax.rem(col_index, flight_tiles) * time_block + col_index // flight_tiles
    dims = (n_row, n_col, scenarios, scen_local, window, tiles, row_tiles, col_tiles)
    vmem = pl.BlockSpec(memory_space=pltpu.VMEM)
    smem = pl.BlockSpec(memory_space=pltpu.SMEM)
    dma = pltpu.SemaphoreType.DMA
    return pl.pallas_call(
        functools.partial(kernel, dims),
        out_shape=(
            jax.ShapeDtypeStruct(increments.shape, F32),
            jax.ShapeDtypeStruct(dual_vars.shape, F32),
        ),
        in_specs=[pl.BlockSpec(memory_space=pl.ANY), smem, smem] + [vmem] * 8,
        out_specs=(vmem, vmem),
        scratch_shapes=[
            pltpu.VMEM((tiles, side, side), BF16),
            pltpu.VMEM((col_tiles, tiles), BF16),
            pltpu.VMEM((row_tiles, tiles), BF16),
            pltpu.VMEM((max(tiles, row_tiles) * scenarios, side), F32),
            pltpu.VMEM((max(col_tiles, row_tiles), scenarios, side), F32),
            pltpu.VMEM((scenarios, col_tiles, side), BF16),
            pltpu.VMEM((devices, scen_local, 16, side), BF16),
            pltpu.VMEM((scen_local, window, flight_local), F32),
            pltpu.VMEM((scen_local, window, flight_local), F32),
            pltpu.VMEM((n_col, scen_local, 16, side), BF16),
            pltpu.VMEM((scenarios, col_tiles, side), BF16),
            pltpu.VMEM((scenarios, row_tiles, side), BF16),
            pltpu.VMEM((n_col, row_tiles, side), BF16),
            pltpu.VMEM((row_tiles, side), F32),
            pltpu.VMEM((row_tiles, side), F32),
            pltpu.VMEM((row_tiles, side), BF16),
            pltpu.VMEM((scenarios, row_tiles, side), BF16),
            dma((LOAD_CHUNKS,)),
            dma((1,)),
            dma((devices,)),
            dma((devices,)),
            dma((devices,)),
            dma((n_col,)),
            dma((n_col,)),
            dma((n_col,)),
        ],
        compiler_params=pltpu.CompilerParams(
            collective_id=0, has_side_effects=True, vmem_limit_bytes=48 * 1024 * 1024
        ),
    )(
        tile_values.reshape(tiles, side, side),
        row_index,
        col_place,
        row_index.reshape(1, tiles),
        col_place.reshape(1, tiles),
        increments,
        dual_vars,
        flight_cost,
        win_start.reshape(1, flight_local),
        win_len.reshape(1, flight_local),
        capacity,
    )


def solution(mesh):
    placed = (
        P("row", "col", None, None, None),
        P("row", "col", None),
        P("row", "col", None),
        P("row", None, "col"),
        P(None, "row"),
        P(None, "col"),
        P("col"),
        P("col"),
        P(None, "row"),
    )
    return jax.shard_map(
        per_device,
        mesh=mesh,
        in_specs=placed,
        out_specs=(P("row", None, "col"), P(None, "row")),
        check_vma=False,
    )
```

time: 668 us -> 176 us (0.26); the launches traced: 659 us -> 175 us
  waiting for transfers between devices: 468 us -> 0 us
  Pallas kernels: 0 us -> 165 us
  local copies, waits for them, and re-layouts: 80.4 us -> 8.01 us
  matrix products: 39.8 us -> 0 us
  blocking collectives: 38 us -> 0 us
  between operations: 14.8 us -> 0.66 us
  other arithmetic: 9.65 us -> 1.38 us
  starting transfers between devices: 8.12 us -> 0 us
    psum x2 -> x0, waiting for transfers between devices: 288 us -> none  [per_device(): col_total = lax.psum(flattened, 'col')]
    pallas_call x0 -> x1, Pallas kernels: none -> 165 us  [per_device(): pl.pallas_call(functools.partial(kernel, dims), out_shape=(jax.ShapeDtype...]
    reduce_scatter x2 -> x0, waiting for transfers between devices: 109 us -> none  [per_device(): lax.psum_scatter(jnp.einsum('cn,snj->scj', hot_cols, products, precision=...]
    all_gather x2 -> x0, waiting for transfers between devices: 62.3 us -> none  [per_device(): gathered_part = lax.all_gather(probe_vec, 'row', axis=0, tiled=True)]
    dot_general x13 -> x0, matrix products: 39.8 us -> none  [the longest x2 15.1 us: per_device(): jnp.einsum('nij,snj->sni', blocks, image_picked, preferred_element_type=j...]
    all_to_all x3 -> x0, blocking collectives: 38 us -> none  [the longest x2 22.2 us: per_device(): lax.all_to_all(probe_fc, 'col', split_axis=1, concat_axis=2, tiled=True)]
    unnamed x24 -> x16, local copies, waits for them, and re-layouts: 39.3 us -> 8.01 us
    reshape x8 -> x0, local copies, waits for them, and re-layouts: 16.2 us -> none  [the longest x4 8.76 us: per_device(): slope_tb = summed.reshape(scen_local, time_block, flights)]
  transfers between devices with their start and end apart: 7 -> 0, of which waited for: 7 -> 0; matrix products, arithmetic and copies ran while one was open for 0% -> 0% of each run, Pallas kernels for 0% -> 0%
where the time goes in v1:
time: 176 us; the launch traced here: 175 us
  Pallas kernels  165 us (94%)
  local copies, waits for them, and re-layouts  8.01 us (5%)
    pallas_call x1, Pallas kernels, per_device(): pl.pallas_call(functools.partial(kernel, dims), out_shape=(jax.ShapeDtype...  165 us
    unnamed x16, local copies, waits for them, and re-layouts  8.01 us

profile of v1, /device:TPU:1, one launch (start us, length us, event | category | flops | bytes accessed | tf_op | source)
XLA Modules:
  0.0 175.3 jit_solution(9569930335682940719)
XLA Ops:
  0.6 0.7 multiply_add_fusion.1.col_of
  1.3 0.7 multiply_add_fusion.col_vec
  2.0 0.0 copy-start
  2.0 1.2 copy-done
  3.2 0.0 copy-start.1
  3.2 1.2 copy-done.1
  4.5 0.0 copy-start.2
  4.5 0.9 copy-done.2
  5.4 0.0 copy-start.3
  5.4 0.9 copy-done.3
  6.3 0.0 copy-start.4
  6.3 0.7 copy-done.4
  7.0 0.0 copy-start.5
  7.0 0.7 copy-done.5
  7.7 0.0 copy-start.6
  7.7 0.7 copy-done.6
  8.4 165.3 %shard_map.104 = (f32[2,128,256]{2,1,0:T(8,128)S(1)}, f32[16,16384]{1,0:T(8,128)S(1)}) custom-call(bf16[256,128,128]{2,1,0:T(8,128)(2,1)} %bitcast.23, s32[256]{0:T(256)S(1)} %bitcast.19, s32[256]{0:T(256)S(1)} %multiply_add_fusion.1.col_of, s32[1,256]{1,0:T(1,128)S(1)} %bitcast.20, s32[1,256]{1,0:T(1,128)S(1)} %multiply_add_fusion.col_vec, ...), custom_call_target="tpu_custom_call" | custom-call | tf_op jit(solution)/shard_map/pallas_call | solution.py:421
  173.6 0.7 copy.13
  174.4 1.0 copy.14
Async XLA Ops:
  2.0 1.2 copy-start
  3.2 1.2 copy-start.1
  4.5 0.9 copy-start.2
  5.4 0.9 copy-start.3
  6.3 0.7 copy-start.4
  7.0 0.7 copy-start.5
  7.7 0.7 copy-start.6

commit v2 on v0

v2 whole, which is shorter than its diff:
```python
import functools
import math
import types

import jax
import jax.numpy as jnp
from jax import lax
from jax.experimental import pallas as pl
from jax.experimental.pallas import tpu as pltpu
from jax.sharding import PartitionSpec as P

ITERS = 2
SIGMA_STEP = 0.2
PARTS = 2
GROUP = 32
MESH = pl.DeviceIdType.MESH
F32, BF16 = jnp.float32, jnp.bfloat16


def kernel(dims, names, *refs):
    n_row, n_col, scenarios, scen_local, window, tiles, row_tiles, col_tiles = dims
    ref = types.SimpleNamespace(**dict(zip(names, refs)))
    devices = n_row * n_col
    scen_part, local_part = scenarios // PARTS, scen_local // PARTS
    half_rows = row_tiles // 2
    block_rows = 16
    flights = ref.inc.shape[2]
    flight_tiles = flights * n_col // 128
    tau_step = 0.6 / math.sqrt(window)
    me_r, me_c = lax.axis_index("row"), lax.axis_index("col")
    me = me_r * n_col + me_c
    me_chip, me_core = me_c // 2, lax.rem(me_c, 2)
    parts = range(PARTS)

    def of_part(name):
        return [getattr(ref, f"{name}{part}") for part in parts]

    by_tile, slope_send, slope_recv = of_part("by_tile"), of_part("slope_send"), of_part("slope_recv")
    probe_send, probe_recv = of_part("probe_send"), of_part("probe_recv")
    image_send, image_recv = of_part("image_send"), of_part("image_recv")
    duals_recv = of_part("duals_recv")
    by_row = [b.reshape(b.shape[0] * b.shape[1], b.shape[2]) for b in by_tile]
    products = ref.products
    flat = products.reshape(products.shape[0] * products.shape[1], products.shape[2])

    def scenario_of(part, position):
        if PARTS == 1:
            return position
        return scen_local * position + part

    def load(source, target, index):
        return pltpu.make_async_copy(source, target, ref.load_sem.at[index])

    cap_lanes = pl.ds(pl.multiple_of(me_core * half_rows * 128, half_rows * 128), half_rows * 128)
    loads = [
        load(ref.dual_hbm, ref.dual_in, 0),
        load(ref.rows_hbm, ref.row_of, 1),
        load(ref.cols_hbm, ref.col_of, 2),
        load(ref.rows_hbm, ref.row_vec, 3),
        load(ref.cols_hbm, ref.col_vec, 4),
        load(ref.inc_hbm, ref.inc, 5),
        load(ref.cost_hbm, ref.cost, 6),
        load(ref.start_hbm, ref.start, 7),
        load(ref.len_hbm, ref.len, 8),
        load(ref.cap_hbm.at[:, cap_lanes], ref.cap_in, 9),
    ]

    def load_blocks(chunk):
        span = pl.ds(chunk * GROUP, GROUP)
        return pltpu.make_async_copy(
            ref.values_hbm.at[span], ref.blocks.at[span], ref.block_sem.at[chunk]
        )

    for copy in loads[:5]:
        copy.start()
    for chunk in range(tiles // GROUP):
        load_blocks(chunk).start()
    for copy in loads[5:]:
        copy.start()

    def peer_of(step):
        peer = lax.rem(me + step, devices)
        return peer // n_col, lax.rem(peer, n_col)

    barrier = pltpu.get_barrier_semaphore()

    @pl.loop(1, devices)
    def _(step):
        pl.semaphore_signal(barrier, inc=1, device_id=peer_of(step), device_id_type=MESH)

    def remote(source, target, send_sem, recv_sem, peer):
        return pltpu.make_async_remote_copy(
            src_ref=source,
            dst_ref=target,
            send_sem=send_sem,
            recv_sem=recv_sem,
            device_id=peer,
            device_id_type=MESH,
        )

    def place(buffer, r, c):
        return buffer.at[
            pl.ds(r * local_part, local_part),
            pl.ds(pl.multiple_of(c * block_rows, block_rows), block_rows),
        ]

    def slope_copy(part, peer):
        return remote(
            place(slope_send[part], *peer),
            slope_recv[part].at[me],
            ref.slope_send_sem.at[part],
            ref.slope_sem.at[part],
            peer,
        )

    def probe_copy(part, peer):
        return remote(
            probe_send[part].at[peer[1]],
            place(probe_recv[part], me_r, me_c),
            ref.probe_send_sem.at[part],
            ref.probe_sem.at[part],
            peer,
        )

    def all_blocks(part, send_sem, recv_sem):
        span = slope_recv[part].at[pl.ds(0, devices - 1)]
        return remote(span, span, send_sem.at[part], recv_sem.at[part], peer_of(1))

    def own_place(buffer, c):
        return buffer.at[
            pl.ds((c // 2) * local_part, local_part),
            pl.ds(pl.multiple_of(lax.rem(c, 2) * half_rows, half_rows), half_rows),
        ]

    def image_copy(part, step):
        peer_c = lax.rem(me_c + step, n_col)
        return remote(
            own_place(image_send[part], peer_c),
            image_recv[part].at[n_col - 1 - step],
            ref.image_send_sem.at[part],
            ref.image_sem.at[part],
            (me_r, peer_c),
        )

    def dual_copy(part, step):
        peer_c = lax.rem(me_c + step, n_col)
        return remote(
            own_place(duals_recv[part], me_c),
            own_place(duals_recv[part], me_c),
            ref.dual_send_sem.at[part],
            ref.dual_sem.at[part],
            (me_r, peer_c),
        )

    def all_rows(part, send_sem, recv_sem):
        span = image_recv[part]
        return remote(
            span, span, send_sem.at[part], recv_sem.at[part], (me_r, lax.rem(me_c + 1, n_col))
        )

    def total(triangle, values):
        return jnp.dot(
            triangle, values, precision=lax.Precision.HIGHEST, preferred_element_type=F32
        )

    def pair(part, index_of, n, transposed):
        left = jnp.concatenate(
            [by_tile[part][index_of(n)], by_tile[part][index_of(n + 1)]], axis=0
        ).astype(BF16)
        if transposed:
            right = ref.blocks[pl.ds(n, 2)].reshape(256, 128)
            contract = (((1,), (1,)), ((), ()))
        else:
            right = jnp.concatenate([ref.blocks[n], ref.blocks[n + 1]], axis=1)
            contract = (((1,), (0,)), ((), ()))
        both = lax.dot_general(left, right, contract, preferred_element_type=F32)
        products[n] = both[:scen_part, :128]
        products[n + 1] = both[scen_part:, 128:]

    def row_index(n):
        return ref.row_of[0, n]

    def col_index(n):
        tile = ref.col_of[0, n]
        return lax.rem(tile, flight_tiles) * 8 + tile // flight_tiles

    def multiply(part, index_of, transposed, loading=False):
        @pl.loop(0, tiles // GROUP)
        def _(group):
            if loading:
                load_blocks(group).wait()
            for k in range(0, GROUP, 2):
                pair(part, index_of, group * GROUP + k, transposed)

    def gathered(hot, position):
        both = jnp.concatenate(
            [flat[pl.ds(position + k, tiles, stride=scen_part), :] for k in range(2)], axis=1
        )
        high = both.astype(BF16)
        low = (both - high.astype(F32)).astype(BF16)
        return jnp.dot(
            hot[...], jnp.concatenate([high, low], axis=0), preferred_element_type=F32
        )

    def send_slope(part, sweep):
        if sweep:
            all_blocks(part, ref.slope_send_sem, ref.slope_sem).wait_send()
        for position in range(0, scen_part, 2):
            summed = gathered(ref.hot_cols, position).astype(BF16)
            slope_send[part][position] = summed[:, :128]
            slope_send[part][position + 1] = summed[:, 128:]
        if sweep == 0 and part == 0:
            pl.semaphore_wait(barrier, devices - 1)

        @pl.loop(1, devices)
        def _(step):
            slope_copy(part, peer_of(step)).start()

        slope_recv[part][me] = place(slope_send[part], me_r, me_c)[...]

    def update_primal(part, sweep, upper, running, trailing):
        all_blocks(part, ref.slope_send_sem, ref.slope_sem).wait_recv()

        @pl.loop(0, n_col)
        def _(block):
            summed = slope_recv[part][block].astype(F32)
            for group in range(1, n_row):
                summed = summed + slope_recv[part][group * n_col + block].astype(F32)
            rows = pl.ds(pl.multiple_of(block * 8, 8), 8)
            for k in range(local_part):
                for half in range(flights // 128):
                    lanes = slice(half * 128, (half + 1) * 128)
                    ref.slope[k, rows, lanes] = (
                        summed[k, half * 8 : (half + 1) * 8] + ref.cost[rows, lanes]
                    )

        if sweep:
            all_blocks(part, ref.probe_send_sem, ref.probe_sem).wait_send()
        for k in range(local_part):
            scen = part * local_part + k
            before = ref.inc if sweep == 0 else ref.primal
            gradient = total(trailing, ref.slope[k])
            fresh = jnp.clip(before[scen] - tau_step * gradient, 0.0, upper)
            ref.primal[scen] = fresh
            fresh_sum = total(running, fresh)
            probe = 2.0 * fresh_sum - ref.cumulative[scen]
            ref.cumulative[scen] = fresh_sum
            for block in range(n_col):
                probe_send[part][block, k] = jnp.concatenate(
                    [
                        probe[block * 8 : (block + 1) * 8, half * 128 : (half + 1) * 128]
                        for half in range(flights // 128)
                    ],
                    axis=0,
                ).astype(BF16)

        @pl.loop(1, devices)
        def _(step):
            probe_copy(part, peer_of(step)).start()

        place(probe_recv[part], me_r, me_c)[...] = probe_send[part][me_c]

    def send_image(part, sweep):
        all_blocks(part, ref.probe_send_sem, ref.probe_sem).wait_recv()
        for position in range(scen_part):
            by_row[part][pl.ds(position, col_tiles, stride=scen_part), :] = probe_recv[part][
                position
            ].astype(F32)
        multiply(part, col_index, True)
        if sweep:
            all_rows(part, ref.image_send_sem, ref.image_sem).wait_send()
        for position in range(0, scen_part, 2):
            summed = gathered(ref.hot_rows, position).astype(BF16)
            image_send[part][position] = summed[:, :128]
            image_send[part][position + 1] = summed[:, 128:]

        @pl.loop(1, n_col)
        def _(step):
            image_copy(part, step).start()

    def update_duals(part, sweep):
        all_rows(part, ref.image_send_sem, ref.image_sem).wait_recv()
        image = own_place(image_send[part], me_c)[...].astype(F32)
        for block in range(n_col - 1):
            image = image + image_recv[part][block].astype(F32)
        updated = jnp.maximum(
            ref.own_dual[part] + SIGMA_STEP * (image - ref.own_cap[part]), 0.0
        )
        ref.own_dual[part] = updated
        if sweep:
            all_rows(part, ref.dual_send_sem, ref.dual_sem).wait_send()
        own_place(duals_recv[part], me_c)[...] = updated.astype(BF16)

        @pl.loop(1, n_col)
        def _(step):
            dual_copy(part, step).start()

    def receive_duals(part):
        all_rows(part, ref.dual_send_sem, ref.dual_sem).wait_recv()

    loads[0].wait()

    @pl.loop(0, row_tiles // 8)
    def _(group):
        for k in range(8):
            tile = group * 8 + k
            ref.staged[pl.ds(pl.multiple_of(tile * scenarios, scenarios), scenarios), :] = (
                ref.dual_in[:, pl.ds(pl.multiple_of(tile * 128, 128), 128)]
            )

    for part in parts:
        by_row[part][0 : row_tiles * scen_part, :] = ref.staged[
            pl.ds(part, row_tiles * scen_part, stride=PARTS), :
        ]
        for k in range(local_part):
            first = me_core * half_rows * scenarios + scenario_of(part, me_chip * local_part + k)
            ref.own_dual[part, k] = ref.staged[pl.ds(first, half_rows, stride=scenarios), :]
    for copy in loads[1:5]:
        copy.wait()
    where_col = lax.rem(ref.col_vec[...], flight_tiles) * 8 + ref.col_vec[...] // flight_tiles
    hot = (where_col == lax.broadcasted_iota(jnp.int32, (col_tiles, tiles), 0)).astype(F32)
    ref.hot_cols[...] = jnp.concatenate([hot, hot], axis=1).astype(BF16)

    for part in parts:
        multiply(part, row_index, False, loading=part == 0)
        send_slope(part, 0)

    hot = (
        ref.row_vec[...] == lax.broadcasted_iota(jnp.int32, (row_tiles, tiles), 0)
    ).astype(F32)
    ref.hot_rows[...] = jnp.concatenate([hot, hot], axis=1).astype(BF16)
    for copy in loads[5:]:
        copy.wait()

    @pl.loop(0, half_rows // 8)
    def _(group):
        for k in range(8):
            tile = group * 8 + k
            ref.staged[pl.ds(pl.multiple_of(tile * scenarios, scenarios), scenarios), :] = (
                ref.cap_in[:, pl.ds(pl.multiple_of(tile * 128, 128), 128)].astype(F32)
            )

    for part in parts:
        for k in range(local_part):
            first = scenario_of(part, me_chip * local_part + k)
            ref.own_cap[part, k] = ref.staged[pl.ds(first, half_rows, stride=scenarios), :]

    row_iota = lax.broadcasted_iota(jnp.int32, (window, window), 0)
    col_iota = lax.broadcasted_iota(jnp.int32, (window, window), 1)
    running = (row_iota >= col_iota).astype(F32)
    trailing = (row_iota <= col_iota).astype(F32)
    for scen in range(scen_local):
        ref.cumulative[scen] = total(running, ref.inc[scen])
    minutes = lax.broadcasted_iota(jnp.int32, (window, flights), 0)
    upper = (
        (minutes >= ref.start[...]) & (minutes < ref.start[...] + ref.len[...])
    ).astype(F32)

    for sweep in range(ITERS):
        for part in parts:
            update_primal(part, sweep, upper, running, trailing)
        for part in parts:
            send_image(part, sweep)
        for part in parts:
            update_duals(part, sweep)
        for part in parts:
            receive_duals(part)
            for position in range(scen_part):
                if sweep < ITERS - 1:
                    target, rows = by_row[part], pl.ds(position, row_tiles, stride=scen_part)
                else:
                    target = ref.staged
                    rows = pl.ds(scenario_of(part, position), row_tiles, stride=scenarios)
                target[rows, :] = duals_recv[part][position].astype(F32)
            if sweep < ITERS - 1:
                multiply(part, row_index, False)
                send_slope(part, sweep + 1)

    @pl.loop(0, row_tiles // 8)
    def _(group):
        for k in range(8):
            tile = group * 8 + k
            ref.duals[:, pl.ds(pl.multiple_of(tile * 128, 128), 128)] = ref.staged[
                pl.ds(pl.multiple_of(tile * scenarios, scenarios), scenarios), :
            ]

    for part in parts:
        all_blocks(part, ref.slope_send_sem, ref.slope_sem).wait_send()
        all_blocks(part, ref.probe_send_sem, ref.probe_sem).wait_send()
        all_rows(part, ref.image_send_sem, ref.image_sem).wait_send()
        all_rows(part, ref.dual_send_sem, ref.dual_sem).wait_send()


def per_device(
    tile_values,
    tile_rows,
    tile_cols,
    increments,
    dual_vars,
    flight_cost,
    win_start,
    win_len,
    capacity,
):
    n_row, n_col = lax.axis_size("row"), lax.axis_size("col")
    tiles, side = tile_values.shape[2], tile_values.shape[3]
    scen_local, window, flight_local = increments.shape
    scenarios, row_length = dual_vars.shape
    row_tiles = row_length // side
    time_block = window // n_col
    col_tiles = time_block * flight_local * n_col // side
    devices = n_row * n_col
    scen_part, local_part = scenarios // PARTS, scen_local // PARTS
    assert side == 128 and time_block == 8 and flight_local == 256
    assert scenarios == n_col and scen_local == 2
    dims = (n_row, n_col, scenarios, scen_local, window, tiles, row_tiles, col_tiles)
    vmem = pl.BlockSpec(memory_space=pltpu.VMEM)
    inputs = dict(
        values_hbm=tile_values.reshape(tiles, side, side),
        rows_hbm=tile_rows.reshape(1, tiles),
        cols_hbm=tile_cols.reshape(1, tiles),
        inc_hbm=increments,
        dual_hbm=dual_vars,
        cost_hbm=flight_cost,
        start_hbm=win_start.reshape(1, flight_local),
        len_hbm=win_len.reshape(1, flight_local),
        cap_hbm=capacity,
    )
    dma = pltpu.SemaphoreType.DMA
    scratch = dict(
        row_of=pltpu.SMEM((1, tiles), jnp.int32),
        col_of=pltpu.SMEM((1, tiles), jnp.int32),
        row_vec=pltpu.VMEM((1, tiles), jnp.int32),
        col_vec=pltpu.VMEM((1, tiles), jnp.int32),
        inc=pltpu.VMEM(increments.shape, F32),
        dual_in=pltpu.VMEM(dual_vars.shape, F32),
        cost=pltpu.VMEM(flight_cost.shape, F32),
        start=pltpu.VMEM((1, flight_local), jnp.int32),
        len=pltpu.VMEM((1, flight_local), jnp.int32),
        cap_in=pltpu.VMEM((scenarios, row_length // 2), jnp.int32),
        blocks=pltpu.VMEM((tiles, side, side), BF16),
        hot_cols=pltpu.VMEM((col_tiles, 2 * tiles), BF16),
        hot_rows=pltpu.VMEM((row_tiles, 2 * tiles), BF16),
        products=pltpu.VMEM((tiles, scen_part, side), F32),
        staged=pltpu.VMEM((row_tiles * scenarios, side), F32),
        slope=pltpu.VMEM((local_part, window, flight_local), F32),
        cumulative=pltpu.VMEM(increments.shape, F32),
        own_dual=pltpu.VMEM((PARTS, local_part, row_tiles // 2, side), F32),
        own_cap=pltpu.VMEM((PARTS, local_part, row_tiles // 2, side), F32),
        load_sem=dma((10,)),
        block_sem=dma((tiles // GROUP,)),
        slope_send_sem=dma((PARTS,)),
        slope_sem=dma((PARTS,)),
        probe_send_sem=dma((PARTS,)),
        probe_sem=dma((PARTS,)),
        image_send_sem=dma((PARTS,)),
        image_sem=dma((PARTS,)),
        dual_send_sem=dma((PARTS,)),
        dual_sem=dma((PARTS,)),
    )
    for part in range(PARTS):
        scratch.update(
            {
                f"by_tile{part}": pltpu.VMEM((max(col_tiles, row_tiles), scen_part, side), F32),
                f"slope_send{part}": pltpu.VMEM((scen_part, col_tiles, side), BF16),
                f"slope_recv{part}": pltpu.VMEM((devices, local_part, 16, side), BF16),
                f"probe_send{part}": pltpu.VMEM((n_col, local_part, 16, side), BF16),
                f"probe_recv{part}": pltpu.VMEM((scen_part, col_tiles, side), BF16),
                f"image_send{part}": pltpu.VMEM((scen_part, row_tiles, side), BF16),
                f"image_recv{part}": pltpu.VMEM((n_col - 1, local_part, row_tiles // 2, side), BF16),
                f"duals_recv{part}": pltpu.VMEM((scen_part, row_tiles, side), BF16),
            }
        )
    names = tuple(inputs) + ("primal", "duals") + tuple(scratch)
    return pl.pallas_call(
        functools.partial(kernel, dims, names),
        out_shape=(
            jax.ShapeDtypeStruct(increments.shape, F32),
            jax.ShapeDtypeStruct(dual_vars.shape, F32),
        ),
        in_specs=[pl.BlockSpec(memory_space=pl.ANY)] * len(inputs),
        out_specs=(vmem, vmem),
        scratch_shapes=list(scratch.values()),
        compiler_params=pltpu.CompilerParams(
            collective_id=0, has_side_effects=True, vmem_limit_bytes=56 * 1024 * 1024
        ),
    )(*inputs.values())


def solution(mesh):
    placed = (
        P("row", "col", None, None, None),
        P("row", "col", None),
        P("row", "col", None),
        P("row", None, "col"),
        P(None, "row"),
        P(None, "col"),
        P("col"),
        P("col"),
        P(None, "row"),
    )
    return jax.shard_map(
        per_device,
        mesh=mesh,
        in_specs=placed,
        out_specs=(P("row", None, "col"), P(None, "row")),
        check_vma=False,
    )
```

time: 668 us -> 111 us (0.17); the launches traced: 659 us -> 110 us
  waiting for transfers between devices: 468 us -> 0 us
  Pallas kernels: 0 us -> 106 us
  local copies, waits for them, and re-layouts: 80.4 us -> 3.93 us
  matrix products: 39.8 us -> 0 us
  blocking collectives: 38 us -> 0 us
  between operations: 14.8 us -> 0.64 us
  other arithmetic: 9.65 us -> 0 us
  starting transfers between devices: 8.12 us -> 0 us
    psum x2 -> x0, waiting for transfers between devices: 288 us -> none  [per_device(): col_total = lax.psum(flattened, 'col')]
    reduce_scatter x2 -> x0, waiting for transfers between devices: 109 us -> none  [per_device(): lax.psum_scatter(jnp.einsum('cn,snj->scj', hot_cols, products, precision=...]
    pallas_call x0 -> x1, Pallas kernels: none -> 106 us  [per_device(): pl.pallas_call(functools.partial(kernel, dims, names), out_shape=(jax.Sha...]
    all_gather x2 -> x0, waiting for transfers between devices: 62.3 us -> none  [per_device(): gathered_part = lax.all_gather(probe_vec, 'row', axis=0, tiled=True)]
    dot_general x13 -> x0, matrix products: 39.8 us -> none  [the longest x2 15.1 us: per_device(): jnp.einsum('nij,snj->sni', blocks, image_picked, preferred_element_type=j...]
    all_to_all x3 -> x0, blocking collectives: 38 us -> none  [the longest x2 22.2 us: per_device(): lax.all_to_all(probe_fc, 'col', split_axis=1, concat_axis=2, tiled=True)]
    unnamed x24 -> x2, local copies, waits for them, and re-layouts: 39.3 us -> 3.93 us
    reshape x8 -> x0, local copies, waits for them, and re-layouts: 16.2 us -> none  [the longest x4 8.76 us: per_device(): slope_tb = summed.reshape(scen_local, time_block, flights)]
  transfers between devices with their start and end apart: 7 -> 0, of which waited for: 7 -> 0; matrix products, arithmetic and copies ran while one was open for 0% -> 0% of each run, Pallas kernels for 0% -> 0%
where the time goes in v2:
time: 111 us; the launch traced here: 110 us
  Pallas kernels  106 us (95%)
  local copies, waits for them, and re-layouts  3.93 us (4%)
    pallas_call x1, Pallas kernels, per_device(): pl.pallas_call(functools.partial(kernel, dims, names), out_shape=(jax.Sha...  106 us
    unnamed x2, local copies, waits for them, and re-layouts  3.93 us

profile of v2, /device:TPU:1, one launch (start us, length us, event | category | flops | bytes accessed | tf_op | source)
XLA Modules:
  0.0 110.4 jit_solution(7577879557620192141)
XLA Ops:
  0.6 105.8 %shard_map.104 = (f32[2,128,256]{2,1,0:T(8,128)}, f32[16,16384]{1,0:T(8,128)}) custom-call(bf16[256,128,128]{2,1,0:T(8,128)(2,1)} %bitcast.5, s32[1,256]{1,0:T(1,128)} %bitcast.6, s32[1,256]{1,0:T(1,128)} %bitcast.7, f32[2,128,256]{2,1,0:T(8,128)} %refs_3_.1, f32[16,16384]{1,0:T(8,128)} %refs_4_.1, f32[128,256]{1,0:T(8,128)} %refs_5_.1, s32[1,256]{1,0:T(1,128)} %bitcast.8, ...), custom_call_target="tpu_custom_call" | custom-call | tf_op jit(solution)/shard_map/pallas_call | solution.py:475
  106.4 1.7 %copy.13 = f32[2,128,256]{2,1,0:T(8,128)} copy(f32[2,128,256]{2,1,0:T(8,128)} %get-tuple-element.4) | data formatting | bytes 524288
  108.1 2.3 %copy.14 = f32[16,16384]{1,0:T(8,128)} copy(f32[16,16384]{1,0:T(8,128)} %get-tuple-element.5) | data formatting | bytes 2097152

commit v3 on v2

--- a/solution.py
+++ b/solution.py
@@ -1,4 +1,5 @@
 import functools
+import itertools
 import math
 import types
 
@@ -12,7 +13,7 @@
 ITERS = 2
 SIGMA_STEP = 0.2
 PARTS = 2
-GROUP = 32
+GROUP = 64
 MESH = pl.DeviceIdType.MESH
 F32, BF16 = jnp.float32, jnp.bfloat16
 
@@ -30,6 +31,7 @@
     me_r, me_c = lax.axis_index("row"), lax.axis_index("col")
     me = me_r * n_col + me_c
     me_chip, me_core = me_c // 2, lax.rem(me_c, 2)
+    assert (n_row, n_col) == (8, 16)
     parts = range(PARTS)
 
     def of_part(name):
@@ -78,15 +80,38 @@
     for copy in loads[5:]:
         copy.start()
 
-    def peer_of(step):
-        peer = lax.rem(me + step, devices)
-        return peer // n_col, lax.rem(peer, n_col)
+    me_z, me_y = me_r // 2, lax.rem(me_chip, 4)
+    me_x = (me_chip // 4) * 2 + lax.rem(me_r, 2)
+    along_x = [lax.rem(me_x + d, 4) for d in range(4)]
+    row_z = [lax.rem(me_z + d, 4) * 2 for d in range(4)]
+    row_x = [lax.rem(x, 2) for x in along_x]
+    col_x = [(x // 2) * 8 for x in along_x]
+    col_y = [lax.rem(me_y + d, 4) * 2 for d in range(4)]
+    col_core = [me_core, 1 - me_core]
+
+    def hops(offset):
+        return sum(min(d, 4 - d) for d in offset[:-1]) + offset[-1] / 8
+
+    def farthest_first(*sizes):
+        return sorted(itertools.product(*map(range, sizes)), key=hops, reverse=True)[:-1]
+
+    every_peer = [
+        (row_z[dz] + row_x[dx], col_x[dx] + col_y[dy] + col_core[dc])
+        for dz, dx, dy, dc in farthest_first(4, 4, 4, 2)
+    ]
+    row_peers = [
+        (me_r, col_x[dx] + col_y[dy] + col_core[dc])
+        for dx, dy, dc in sorted(
+            ((2 * far, dy, dc) for far in range(2) for dy in range(4) for dc in range(2)),
+            key=hops,
+            reverse=True,
+        )[:-1]
+    ]
 
     barrier = pltpu.get_barrier_semaphore()
 
-    @pl.loop(1, devices)
-    def _(step):
-        pl.semaphore_signal(barrier, inc=1, device_id=peer_of(step), device_id_type=MESH)
+    for peer in every_peer:
+        pl.semaphore_signal(barrier, inc=1, device_id=peer, device_id_type=MESH)
 
     def remote(source, target, send_sem, recv_sem, peer):
         return pltpu.make_async_remote_copy(
@@ -124,7 +149,7 @@
 
     def all_blocks(part, send_sem, recv_sem):
         span = slope_recv[part].at[pl.ds(0, devices - 1)]
-        return remote(span, span, send_sem.at[part], recv_sem.at[part], peer_of(1))
+        return remote(span, span, send_sem.at[part], recv_sem.at[part], every_peer[0])
 
     def own_place(buffer, c):
         return buffer.at[
@@ -132,31 +157,27 @@
             pl.ds(pl.multiple_of(lax.rem(c, 2) * half_rows, half_rows), half_rows),
         ]
 
-    def image_copy(part, step):
-        peer_c = lax.rem(me_c + step, n_col)
+    def image_copy(part, index):
         return remote(
-            own_place(image_send[part], peer_c),
-            image_recv[part].at[n_col - 1 - step],
+            own_place(image_send[part], row_peers[index][1]),
+            image_recv[part].at[index],
             ref.image_send_sem.at[part],
             ref.image_sem.at[part],
-            (me_r, peer_c),
-        )
-
-    def dual_copy(part, step):
-        peer_c = lax.rem(me_c + step, n_col)
+            row_peers[index],
+        )
+
+    def dual_copy(part, index):
         return remote(
             own_place(duals_recv[part], me_c),
             own_place(duals_recv[part], me_c),
             ref.dual_send_sem.at[part],
             ref.dual_sem.at[part],
-            (me_r, peer_c),
+            row_peers[index],
         )
 
     def all_rows(part, send_sem, recv_sem):
         span = image_recv[part]
-        return remote(
-            span, span, send_sem.at[part], recv_sem.at[part], (me_r, lax.rem(me_c + 1, n_col))
-        )
+        return remote(span, span, send_sem.at[part], recv_sem.at[part], row_peers[0])
 
     def total(triangle, values):
         return jnp.dot(
@@ -202,20 +223,17 @@
             hot[...], jnp.concatenate([high, low], axis=0), preferred_element_type=F32
         )
 
-    def send_slope(part, sweep):
+    def fold_slope(part, sweep):
         if sweep:
             all_blocks(part, ref.slope_send_sem, ref.slope_sem).wait_send()
         for position in range(0, scen_part, 2):
             summed = gathered(ref.hot_cols, position).astype(BF16)
             slope_send[part][position] = summed[:, :128]
             slope_send[part][position + 1] = summed[:, 128:]
-        if sweep == 0 and part == 0:
-            pl.semaphore_wait(barrier, devices - 1)
-
-        @pl.loop(1, devices)
-        def _(step):
-            slope_copy(part, peer_of(step)).start()
-
+
+    def send_slope(part):
+        for peer in every_peer:
+            slope_copy(part, peer).start()
         slope_recv[part][me] = place(slope_send[part], me_r, me_c)[...]
 
     def update_primal(part, sweep, upper, running, trailing):
@@ -254,9 +272,8 @@
                     axis=0,
                 ).astype(BF16)
 
-        @pl.loop(1, devices)
-        def _(step):
-            probe_copy(part, peer_of(step)).start()
+        for peer in every_peer:
+            probe_copy(part, peer).start()
 
         place(probe_recv[part], me_r, me_c)[...] = probe_send[part][me_c]
 
@@ -274,9 +291,8 @@
             image_send[part][position] = summed[:, :128]
             image_send[part][position + 1] = summed[:, 128:]
 
-        @pl.loop(1, n_col)
-        def _(step):
-            image_copy(part, step).start()
+        for index in range(n_col - 1):
+            image_copy(part, index).start()
 
     def update_duals(part, sweep):
         all_rows(part, ref.image_send_sem, ref.image_sem).wait_recv()
@@ -291,9 +307,8 @@
             all_rows(part, ref.dual_send_sem, ref.dual_sem).wait_send()
         own_place(duals_recv[part], me_c)[...] = updated.astype(BF16)
 
-        @pl.loop(1, n_col)
-        def _(step):
-            dual_copy(part, step).start()
+        for index in range(n_col - 1):
+            dual_copy(part, index).start()
 
     def receive_duals(part):
         all_rows(part, ref.dual_send_sem, ref.dual_sem).wait_recv()
@@ -323,7 +338,10 @@
 
     for part in parts:
         multiply(part, row_index, False, loading=part == 0)
-        send_slope(part, 0)
+        fold_slope(part, 0)
+        if part == 0:
+            pl.semaphore_wait(barrier, devices - 1)
+        send_slope(part)
 
     hot = (
         ref.row_vec[...] == lax.broadcasted_iota(jnp.int32, (row_tiles, tiles), 0)
@@ -374,7 +392,8 @@
                 target[rows, :] = duals_recv[part][position].astype(F32)
             if sweep < ITERS - 1:
                 multiply(part, row_index, False)
-                send_slope(part, sweep + 1)
+                fold_slope(part, sweep + 1)
+                send_slope(part)
 
     @pl.loop(0, row_tiles // 8)
     def _(group):

time: 111 us -> 101 us (0.910)
  Pallas kernels: 106 us -> 96.7 us
    pallas_call x1, Pallas kernels: 106 us -> 96.7 us  [per_device(): pl.pallas_call(functools.partial(kernel, dims, names), out_shape=(jax.Sha...]
where the time goes in v3:
time: 101 us
  Pallas kernels  96.7 us (96%)
  local copies, waits for them, and re-layouts  3.93 us (4%)
    pallas_call x1, Pallas kernels, per_device(): pl.pallas_call(functools.partial(kernel, dims, names), out_shape=(jax.Sha...  96.7 us
    unnamed x2, local copies, waits for them, and re-layouts  3.93 us

profile of v3, /device:TPU:1, one launch (start us, length us, event | category | flops | bytes accessed | tf_op | source)
XLA Modules:
  0.0 101.2 jit_solution(9516639401611521795)
XLA Ops:
  0.6 96.7 %shard_map.104 = (f32[2,128,256]{2,1,0:T(8,128)}, f32[16,16384]{1,0:T(8,128)}) custom-call(bf16[256,128,128]{2,1,0:T(8,128)(2,1)} %bitcast.5, s32[1,256]{1,0:T(1,128)} %bitcast.6, s32[1,256]{1,0:T(1,128)} %bitcast.7, f32[2,128,256]{2,1,0:T(8,128)} %refs_3_.1, f32[16,16384]{1,0:T(8,128)} %refs_4_.1, f32[128,256]{1,0:T(8,128)} %refs_5_.1, s32[1,256]{1,0:T(1,128)} %bitcast.8, ...), custom_call_target="tpu_custom_call" | custom-call | tf_op jit(solution)/shard_map/pallas_call | solution.py:494
  97.3 1.7 %copy.13 = f32[2,128,256]{2,1,0:T(8,128)} copy(f32[2,128,256]{2,1,0:T(8,128)} %get-tuple-element.4) | data formatting | bytes 524288
  99.0 2.3 %copy.14 = f32[16,16384]{1,0:T(8,128)} copy(f32[16,16384]{1,0:T(8,128)} %get-tuple-element.5) | data formatting | bytes 2097152

commit v4 on v3

--- a/solution.py
+++ b/solution.py
@@ -42,8 +42,8 @@
     image_send, image_recv = of_part("image_send"), of_part("image_recv")
     duals_recv = of_part("duals_recv")
     by_row = [b.reshape(b.shape[0] * b.shape[1], b.shape[2]) for b in by_tile]
-    products = ref.products
-    flat = products.reshape(products.shape[0] * products.shape[1], products.shape[2])
+    products = of_part("products")
+    flat = [p.reshape(p.shape[0] * p.shape[1], p.shape[2]) for p in products]
 
     def scenario_of(part, position):
         if PARTS == 1:
@@ -195,8 +195,8 @@
             right = jnp.concatenate([ref.blocks[n], ref.blocks[n + 1]], axis=1)
             contract = (((1,), (0,)), ((), ()))
         both = lax.dot_general(left, right, contract, preferred_element_type=F32)
-        products[n] = both[:scen_part, :128]
-        products[n + 1] = both[scen_part:, 128:]
+        products[part][n] = both[:scen_part, :128]
+        products[part][n + 1] = both[scen_part:, 128:]
 
     def row_index(n):
         return ref.row_of[0, n]
@@ -205,17 +205,33 @@
         tile = ref.col_of[0, n]
         return lax.rem(tile, flight_tiles) * 8 + tile // flight_tiles
 
-    def multiply(part, index_of, transposed, loading=False):
+    def multiply(part, index_of, transposed):
         @pl.loop(0, tiles // GROUP)
         def _(group):
-            if loading:
-                load_blocks(group).wait()
             for k in range(0, GROUP, 2):
                 pair(part, index_of, group * GROUP + k, transposed)
 
-    def gathered(hot, position):
+    def multiply_arriving():
+        @pl.loop(0, tiles // GROUP)
+        def _(group):
+            load_blocks(group).wait()
+            for k in range(0, GROUP, 2):
+                n = group * GROUP + k
+                left = jnp.concatenate(
+                    [by_tile[part][row_index(n + i)] for i in range(2) for part in parts], axis=0
+                ).astype(BF16)
+                right = jnp.concatenate([ref.blocks[n], ref.blocks[n + 1]], axis=1)
+                both = jnp.dot(left, right, preferred_element_type=F32)
+                for i in range(2):
+                    for part in parts:
+                        first = i * scenarios + part * scen_part
+                        products[part][n + i] = both[
+                            first : first + scen_part, i * 128 : (i + 1) * 128
+                        ]
+
+    def gathered(part, hot, position):
         both = jnp.concatenate(
-            [flat[pl.ds(position + k, tiles, stride=scen_part), :] for k in range(2)], axis=1
+            [flat[part][pl.ds(position + k, tiles, stride=scen_part), :] for k in range(2)], axis=1
         )
         high = both.astype(BF16)
         low = (both - high.astype(F32)).astype(BF16)
@@ -227,7 +243,7 @@
         if sweep:
             all_blocks(part, ref.slope_send_sem, ref.slope_sem).wait_send()
         for position in range(0, scen_part, 2):
-            summed = gathered(ref.hot_cols, position).astype(BF16)
+            summed = gathered(part, ref.hot_cols, position).astype(BF16)
             slope_send[part][position] = summed[:, :128]
             slope_send[part][position + 1] = summed[:, 128:]
 
@@ -239,7 +255,7 @@
     def update_primal(part, sweep, upper, running, trailing):
         all_blocks(part, ref.slope_send_sem, ref.slope_sem).wait_recv()
 
-        @pl.loop(0, n_col)
+        @pl.loop(0, n_col, unroll=4)
         def _(block):
             summed = slope_recv[part][block].astype(F32)
             for group in range(1, n_row):
@@ -287,7 +303,7 @@
         if sweep:
             all_rows(part, ref.image_send_sem, ref.image_sem).wait_send()
         for position in range(0, scen_part, 2):
-            summed = gathered(ref.hot_rows, position).astype(BF16)
+            summed = gathered(part, ref.hot_rows, position).astype(BF16)
             image_send[part][position] = summed[:, :128]
             image_send[part][position + 1] = summed[:, 128:]
 
@@ -336,8 +352,8 @@
     hot = (where_col == lax.broadcasted_iota(jnp.int32, (col_tiles, tiles), 0)).astype(F32)
     ref.hot_cols[...] = jnp.concatenate([hot, hot], axis=1).astype(BF16)
 
+    multiply_arriving()
     for part in parts:
-        multiply(part, row_index, False, loading=part == 0)
         fold_slope(part, 0)
         if part == 0:
             pl.semaphore_wait(barrier, devices - 1)
@@ -460,7 +476,6 @@
         blocks=pltpu.VMEM((tiles, side, side), BF16),
         hot_cols=pltpu.VMEM((col_tiles, 2 * tiles), BF16),
         hot_rows=pltpu.VMEM((row_tiles, 2 * tiles), BF16),
-        products=pltpu.VMEM((tiles, scen_part, side), F32),
         staged=pltpu.VMEM((row_tiles * scenarios, side), F32),
         slope=pltpu.VMEM((local_part, window, flight_local), F32),
         cumulative=pltpu.VMEM(increments.shape, F32),
@@ -481,6 +496,7 @@
         scratch.update(
             {
                 f"by_tile{part}": pltpu.VMEM((max(col_tiles, row_tiles), scen_part, side), F32),
+                f"products{part}": pltpu.VMEM((tiles, scen_part, side), F32),
                 f"slope_send{part}": pltpu.VMEM((scen_part, col_tiles, side), BF16),
                 f"slope_recv{part}": pltpu.VMEM((devices, local_part, 16, side), BF16),
                 f"probe_send{part}": pltpu.VMEM((n_col, local_part, 16, side), BF16),

time: 101 us -> 101 us (level)
  no operation moved by 1% of the time
where the time goes in v4:
time: 101 us
  Pallas kernels  96.3 us (95%)
  local copies, waits for them, and re-layouts  3.93 us (4%)
    pallas_call x1, Pallas kernels, per_device(): pl.pallas_call(functools.partial(kernel, dims, names), out_shape=(jax.Sha...  96.3 us
    unnamed x2, local copies, waits for them, and re-layouts  3.93 us

profile of v4, /device:TPU:1, one launch (start us, length us, event | category | flops | bytes accessed | tf_op | source)
XLA Modules:
  0.0 100.9 jit_solution(15917369266581633183)
XLA Ops:
  0.6 96.3 %shard_map.104 = (f32[2,128,256]{2,1,0:T(8,128)}, f32[16,16384]{1,0:T(8,128)}) custom-call(bf16[256,128,128]{2,1,0:T(8,128)(2,1)} %bitcast.5, s32[1,256]{1,0:T(1,128)} %bitcast.6, s32[1,256]{1,0:T(1,128)} %bitcast.7, f32[2,128,256]{2,1,0:T(8,128)} %refs_3_.1, f32[16,16384]{1,0:T(8,128)} %refs_4_.1, f32[128,256]{1,0:T(8,128)} %refs_5_.1, s32[1,256]{1,0:T(1,128)} %bitcast.8, ...), custom_call_target="tpu_custom_call" | custom-call | tf_op jit(solution)/shard_map/pallas_call | solution.py:510
  97.0 1.7 %copy.13 = f32[2,128,256]{2,1,0:T(8,128)} copy(f32[2,128,256]{2,1,0:T(8,128)} %get-tuple-element.4) | data formatting | bytes 524288
  98.7 2.3 %copy.14 = f32[16,16384]{1,0:T(8,128)} copy(f32[16,16384]{1,0:T(8,128)} %get-tuple-element.5) | data formatting | bytes 2097152

commit v5 on v4

--- a/solution.py
+++ b/solution.py
@@ -243,9 +243,18 @@
         if sweep:
             all_blocks(part, ref.slope_send_sem, ref.slope_sem).wait_send()
         for position in range(0, scen_part, 2):
-            summed = gathered(part, ref.hot_cols, position).astype(BF16)
-            slope_send[part][position] = summed[:, :128]
-            slope_send[part][position + 1] = summed[:, 128:]
+            summed = gathered(part, ref.hot_cols, position)
+            ref.shaped[:col_tiles] = summed[:, :128]
+            ref.shaped[col_tiles:] = summed[:, 128:]
+            carried = jnp.zeros((2 * col_tiles // 8, 128), F32)
+            for minute in reversed(range(8)):
+                rows = pl.ds(minute, 2 * col_tiles // 8, stride=8)
+                exact = ref.shaped[rows, :] + carried
+                rounded = exact.astype(BF16).astype(F32)
+                ref.shaped[rows, :] = rounded
+                carried = exact - rounded
+            slope_send[part][position] = ref.shaped[:col_tiles].astype(BF16)
+            slope_send[part][position + 1] = ref.shaped[col_tiles:].astype(BF16)
 
     def send_slope(part):
         for peer in every_peer:
@@ -476,6 +485,7 @@
         blocks=pltpu.VMEM((tiles, side, side), BF16),
         hot_cols=pltpu.VMEM((col_tiles, 2 * tiles), BF16),
         hot_rows=pltpu.VMEM((row_tiles, 2 * tiles), BF16),
+        shaped=pltpu.VMEM((2 * col_tiles, side), F32),
         staged=pltpu.VMEM((row_tiles * scenarios, side), F32),
         slope=pltpu.VMEM((local_part, window, flight_local), F32),
         cumulative=pltpu.VMEM(increments.shape, F32),

time: 101 us -> 103 us (1.020)
  Pallas kernels: 96.3 us -> 98 us
    pallas_call x1, Pallas kernels: 96.3 us -> 98 us  [per_device(): pl.pallas_call(functools.partial(kernel, dims, names), out_shape=(jax.Sha...]
where the time goes in v5:
time: 103 us
  Pallas kernels  98 us (95%)
  local copies, waits for them, and re-layouts  3.93 us (4%)
    pallas_call x1, Pallas kernels, per_device(): pl.pallas_call(functools.partial(kernel, dims, names), out_shape=(jax.Sha...  98 us
    unnamed x2, local copies, waits for them, and re-layouts  3.93 us

profile of v5, /device:TPU:1, one launch (start us, length us, event | category | flops | bytes accessed | tf_op | source)
XLA Modules:
  0.0 102.5 jit_solution(9493396526167279684)
XLA Ops:
  0.6 98.0 %shard_map.104 = (f32[2,128,256]{2,1,0:T(8,128)}, f32[16,16384]{1,0:T(8,128)}) custom-call(bf16[256,128,128]{2,1,0:T(8,128)(2,1)} %bitcast.5, s32[1,256]{1,0:T(1,128)} %bitcast.6, s32[1,256]{1,0:T(1,128)} %bitcast.7, f32[2,128,256]{2,1,0:T(8,128)} %refs_3_.1, f32[16,16384]{1,0:T(8,128)} %refs_4_.1, f32[128,256]{1,0:T(8,128)} %refs_5_.1, s32[1,256]{1,0:T(1,128)} %bitcast.8, ...), custom_call_target="tpu_custom_call" | custom-call | tf_op jit(solution)/shard_map/pallas_call | solution.py:520
  98.6 1.7 %copy.13 = f32[2,128,256]{2,1,0:T(8,128)} copy(f32[2,128,256]{2,1,0:T(8,128)} %get-tuple-element.4) | data formatting | bytes 524288
  100.3 2.3 %copy.14 = f32[16,16384]{1,0:T(8,128)} copy(f32[16,16384]{1,0:T(8,128)} %get-tuple-element.5) | data formatting | bytes 2097152

commit v6 on v4

--- a/solution.py
+++ b/solution.py
@@ -14,6 +14,7 @@
 SIGMA_STEP = 0.2
 PARTS = 2
 GROUP = 64
+UNROLLED = 128
 MESH = pl.DeviceIdType.MESH
 F32, BF16 = jnp.float32, jnp.bfloat16
 
@@ -206,10 +207,10 @@
         return lax.rem(tile, flight_tiles) * 8 + tile // flight_tiles
 
     def multiply(part, index_of, transposed):
-        @pl.loop(0, tiles // GROUP)
+        @pl.loop(0, tiles // UNROLLED)
         def _(group):
-            for k in range(0, GROUP, 2):
-                pair(part, index_of, group * GROUP + k, transposed)
+            for k in range(0, UNROLLED, 2):
+                pair(part, index_of, group * UNROLLED + k, transposed)
 
     def multiply_arriving():
         @pl.loop(0, tiles // GROUP)

time: 101 us -> 100 us (0.990)
  Pallas kernels: 96.3 us -> 95.1 us
    pallas_call x1, Pallas kernels: 96.3 us -> 95.1 us  [per_device(): pl.pallas_call(functools.partial(kernel, dims, names), out_shape=(jax.Sha...]
where the time goes in v6:
time: 100 us; the launch traced here: 99.6 us
  Pallas kernels  95.1 us (95%)
  local copies, waits for them, and re-layouts  3.93 us (4%)
    pallas_call x1, Pallas kernels, per_device(): pl.pallas_call(functools.partial(kernel, dims, names), out_shape=(jax.Sha...  95.1 us
    unnamed x2, local copies, waits for them, and re-layouts  3.93 us

profile of v6, /device:TPU:1, one launch (start us, length us, event | category | flops | bytes accessed | tf_op | source)
XLA Modules:
  0.0 99.6 jit_solution(13655246993349966187)
XLA Ops:
  0.6 95.1 %shard_map.104 = (f32[2,128,256]{2,1,0:T(8,128)}, f32[16,16384]{1,0:T(8,128)}) custom-call(bf16[256,128,128]{2,1,0:T(8,128)(2,1)} %bitcast.5, s32[1,256]{1,0:T(1,128)} %bitcast.6, s32[1,256]{1,0:T(1,128)} %bitcast.7, f32[2,128,256]{2,1,0:T(8,128)} %refs_3_.1, f32[16,16384]{1,0:T(8,128)} %refs_4_.1, f32[128,256]{1,0:T(8,128)} %refs_5_.1, s32[1,256]{1,0:T(1,128)} %bitcast.8, ...), custom_call_target="tpu_custom_call" | custom-call | tf_op jit(solution)/shard_map/pallas_call | solution.py:511
  95.7 1.7 %copy.13 = f32[2,128,256]{2,1,0:T(8,128)} copy(f32[2,128,256]{2,1,0:T(8,128)} %get-tuple-element.4) | data formatting | bytes 524288
  97.4 2.3 %copy.14 = f32[16,16384]{1,0:T(8,128)} copy(f32[16,16384]{1,0:T(8,128)} %get-tuple-element.5) | data formatting | bytes 2097152
